TPU v7x, 256 devices: a whole 4x4x8 slice. The times are simulated.
256 devices in a mesh: row: 8 (over x, core), col: 32 (over y, z).
Axes of the slice: x: 4, y: 4, z: 8, core: 2. Of those that a mesh axis runs over, the one named last changes fastest.
Arguments:
- matrix: float32 [16384, 16384], P('row', 'col'), as said below
- panel: float32 [16384, 256], P(('row', 'col')), may hold values from -0.046875 to 0.046875
- factor: float32 [256, 256], replicated, as said below
Outputs:
- updated: float32 [16384, 16384], P('row', 'col')
- correction: float32 [16384, 256], P(('row', 'col'))
Inputs may be any that keep to these rules, and one draw needn't show every extreme that they name: `matrix`: symmetric. `factor`: upper triangular with a positive diagonal.
All inputs are finite; a program needn't handle non-finite values.
Results may differ from a plain program's by a relative error of at most 0.000071.
Values sent between devices are 32-bit elements; how exact they have to be, the bound alone decides.
No kernel may reach another device: no remote copies, remote signals or barrier semaphores. Data moves between devices by JAX's collectives and lax.ppermute only.
A program may use at most 64 MiB of HBM per device.

v0:
```python
import jax
import jax.numpy as jnp
from jax import lax
from jax.sharding import PartitionSpec as P


def from_root(value, axis, source):
    kept = jnp.where(lax.axis_index(axis) == source, value, 0).astype(value.dtype)
    return lax.psum(kept, axis)


def mult(left, right):
    return jnp.dot(left, right, precision=lax.Precision.HIGHEST, preferred_element_type=jnp.float32)


def per_device(matrix, panel, factor):
    ncols = lax.axis_size("col")
    nrows = lax.axis_size("row")
    blocks = panel.shape[0]
    col_index = lax.axis_index("col")
    col_rows = blocks * nrows
    offset = col_index * nrows % ncols * blocks
    owner = col_index * nrows // ncols
    row_panel = lax.all_gather(panel, "col", axis=0, tiled=True)
    col_panel = from_root(lax.dynamic_slice_in_dim(row_panel, offset, col_rows, 0), "row", owner)
    product = lax.psum_scatter(mult(matrix, col_panel), "col", scatter_dimension=0, tiled=True)
    scaled = mult(product, factor)
    small = lax.psum(mult(panel.T, scaled), ("row", "col"))
    correction = scaled - 0.5 * mult(panel, mult(factor.T, small))
    row_corr = lax.all_gather(correction, "col", axis=0, tiled=True)
    col_corr = from_root(lax.dynamic_slice_in_dim(row_corr, offset, col_rows, 0), "row", owner)
    updated = matrix - mult(row_panel, col_corr.T) - mult(row_corr, col_panel.T)
    return (updated, correction)


def solution(mesh):
    in_specs = (P("row", "col"), P(("row", "col"), None), P())
    out_specs = (P("row", "col"), P(("row", "col"), None))
    return jax.shard_map(
        per_device, mesh=mesh, in_specs=in_specs, out_specs=out_specs, check_vma=False
    )
```

profile of v0, /device:TPU:8, one launch (start us, length us, event | category | flops | bytes accessed | tf_op | source)
XLA Modules:
  0.0 802.7 jit_solution(14840826598810947577)
XLA Ops:
  7.2 0.0 copy-start
  7.2 0.0 all-gather.3.cloned.1.call-start
  7.2 0.7 all-gather.3.cloned.1.call-update
  7.9 0.0 all-reduce.4.cloned.1.call-start
  8.0 82.3 %all-gather.3.cloned.1.call-done = f32[2048,256]{1,0:T(8,128)} async-done(((f32[64,256]{1,0:T(8,128)}), f32[2048,256]{1,0:T(8,128)}) %all-gather.3.cloned.1.call-update) | async-done | bytes 2097168 | tf_op jit(solution)/shard_map/all_gather | solution.py:24
  90.3 1.9 dynamic-slice_select_fusion.1
  92.1 0.0 all-reduce.4.cloned.1.call-update
  92.2 0.0 reduce-scatter.4.cloned.1.call-start
  92.2 65.1 %all-reduce.4.cloned.1.call-done = f32[512,256]{1,0:T(8,128)} async-done(((f32[512,256]{1,0:T(8,128)}), f32[512,256]{1,0:T(8,128)}) %all-reduce.4.cloned.1.call-update) | async-done | bytes 524304 | tf_op jit(solution)/shard_map/psum | solution.py:9
  157.3 8.7 %convolution_bitcast_fusion = f32[2048,256]{0,1:T(8,128)S(1)} fusion(f32[512,256]{1,0:T(8,128)} %all-reduce.4.cloned.1.call-done, f32[2048,512]{1,0:T(8,128)} %param.3), kind=kOutput, calls=%fused_computation.2 | convolution fusion | flops 3221225472 | bytes 6815744 | tf_op jit(solution)/shard_map/dot_general | solution.py:13
  166.0 0.0 copy-start.3
  166.0 1.8 copy.12
  167.8 0.0 reduce-scatter.4.cloned.1.call-update
  167.8 0.0 all-reduce.6.cloned.1.call-start
  167.9 214.8 %reduce-scatter.4.cloned.1.call-done = f32[64,256]{1,0:T(8,128)} async-done(((f32[2048,256]{1,0:T(8,128)}), f32[64,256]{1,0:T(8,128)}) %reduce-scatter.4.cloned.1.call-update) | async-done | bytes 65552
  382.7 0.0 copy-done
  382.7 1.1 fusion.3
  383.8 0.0 copy-done.3
  383.8 1.1 convolution_bitcast_fusion.1
  384.9 0.0 all-reduce.6.cloned.1.call-update
  384.9 0.0 all-gather.5.cloned.1.call-start
  385.0 252.9 %all-reduce.6.cloned.1.call-done = f32[256,256]{0,1:T(8,128)} async-done(((f32[256,256]{0,1:T(8,128)}), f32[256,256]{0,1:T(8,128)}) %all-reduce.6.cloned.1.call-update) | async-done | bytes 262160 | tf_op jit(solution)/shard_map/psum | solution.py:28
  637.9 1.3 fusion.4
  639.2 1.0 fusion.2
  640.3 0.0 all-gather.5.cloned.1.call-update
  640.3 0.0 copy-start.2
  640.3 0.0 all-reduce.8.cloned.1.call-start
  640.3 5.4 copy.8
  645.8 0.0 copy-start.1
  645.8 70.7 %all-gather.5.cloned.1.call-done = f32[2048,256]{1,0:T(8,128)} async-done(((f32[64,256]{1,0:T(8,128)}), f32[2048,256]{1,0:T(8,128)}) %all-gather.5.cloned.1.call-update) | async-done | bytes 2097168 | tf_op jit(solution)/shard_map/all_gather | solution.py:30
  716.5 1.9 dynamic-slice_select_fusion
  718.4 0.0 all-reduce.8.cloned.1.call-update
  718.4 0.0 copy-done.2
  718.4 6.9 fusion.5
  725.3 57.5 %all-reduce.8.cloned.1.call-done = f32[512,256]{1,0:T(8,128)} async-done(((f32[512,256]{1,0:T(8,128)}), f32[512,256]{1,0:T(8,128)}) %all-reduce.8.cloned.1.call-update) | async-done | bytes 524304 | tf_op jit(solution)/shard_map/psum | solution.py:9
  782.8 0.0 copy-done.1
  782.8 7.7 fusion
  790.5 5.3 copy.10
Async XLA Ops:
  7.2 375.5 %copy-start = (f32[256,256]{1,0:T(8,128)S(1)}, f32[256,256]{1,0:T(8,128)}, u32[]{:S(2)}) copy-start(f32[256,256]{1,0:T(8,128)} %param.5) | copy-start | bytes 786436
  7.2 83.1 %all-gather.3.cloned.1.call-start = ((), (), s32[]{:S(2)}) async-start(), calls=%async_computation.1 | async-start | bytes 2162688 | tf_op jit(solution)/shard_map/all_gather | solution.py:24
  7.9 149.4 %all-reduce.4.cloned.1.call-start = ((), (), s32[]{:S(2)}) async-start(), calls=%async_computation.2 | async-start | bytes 1048576 | tf_op jit(solution)/shard_map/psum | solution.py:9
  92.2 290.5 %reduce-scatter.4.cloned.1.call-start = ((), (), s32[]{:S(2)}) async-start(), calls=%async_computation.6 | async-start | bytes 2162688
  166.0 217.8 %copy-start.3 = (f32[64,256]{1,0:T(8,128)S(1)}, f32[64,256]{1,0:T(8,128)}, u32[]{:S(2)}) copy-start(f32[64,256]{1,0:T(8,128)} %param.4) | copy-start | bytes 196612
  167.8 470.1 %all-reduce.6.cloned.1.call-start = ((), (), s32[]{:S(2)}) async-start(), calls=%async_computation.3 | async-start | bytes 524288 | tf_op jit(solution)/shard_map/psum | solution.py:28
  384.9 331.5 %all-gather.5.cloned.1.call-start = ((), (), s32[]{:S(2)}) async-start(), calls=%async_computation.4 | async-start | bytes 2162688 | tf_op jit(solution)/shard_map/all_gather | solution.py:30
  640.3 78.1 %copy-start.2 = (f32[512,256]{1,0:T(8,128)S(1)}, f32[512,256]{1,0:T(8,128)}, u32[]{:S(2)}) copy-start(f32[512,256]{1,0:T(8,128)} %all-reduce.4.cloned.1.call-done) | copy-start | bytes 1572868
  640.3 142.5 %all-reduce.8.cloned.1.call-start = ((), (), s32[]{:S(2)}) async-start(), calls=%async_computation.5 | async-start | bytes 1048576 | tf_op jit(solution)/shard_map/psum | solution.py:9
  645.8 137.0 %copy-start.1 = (f32[2048,256]{1,0:T(8,128)S(1)}, f32[2048,256]{1,0:T(8,128)}, u32[]{:S(2)}) copy-start(f32[2048,256]{1,0:T(8,128)} %all-gather.3.cloned.1.call-done) | copy-start | bytes 6291460
Sparse Core Ops, SparseCore 0:
  10.6 79.6 all-gather.2
  93.2 64.0 all-reduce.3
  168.0 214.6 reduce-scatter.3
  388.6 249.2 all-reduce.5
  640.9 75.5 all-gather.4
  718.7 64.0 all-reduce.7
where the time goes:
time: 803 us
  waiting for transfers between devices  744 us (93%)
  matrix products  27.9 us (3%)
  between operations  14.2 us (2%)
  local copies, waits for them, and re-layouts  12.6 us (2%)
    psum x1, waiting for transfers between devices, per_device(): small = lax.psum(mult(panel.T, scaled), ('row', 'col'))  253 us
    unnamed x7, waiting for transfers between devices  216 us
    psum x2, waiting for transfers between devices, from_root(): return lax.psum(kept, axis)  123 us
    all_gather x1, waiting for transfers between devices, per_device(): row_panel = lax.all_gather(panel, 'col', axis=0, tiled=True)  82.3 us
    all_gather x1, waiting for transfers between devices, per_device(): row_corr = lax.all_gather(correction, 'col', axis=0, tiled=True)  70.7 us
    dot_general x7, matrix products, mult(): jnp.dot(left, right, precision=lax.Precision.HIGHEST, preferred_element_t...  27.9 us
  transfers between devices with their start and end apart: 6, of which 6 were waited for; matrix products, arithmetic and copies ran while one was open for 2% of the time, Pallas kernels for 0%

commit v1 on v0

--- a/solution.py
+++ b/solution.py
@@ -25,7 +25,8 @@
     col_panel = from_root(lax.dynamic_slice_in_dim(row_panel, offset, col_rows, 0), "row", owner)
     product = lax.psum_scatter(mult(matrix, col_panel), "col", scatter_dimension=0, tiled=True)
     scaled = mult(product, factor)
-    small = lax.psum(mult(panel.T, scaled), ("row", "col"))
+    one_axis = lax.psum(mult(panel.T, scaled), "row")
+    small = lax.psum(one_axis, "col")
     correction = scaled - 0.5 * mult(panel, mult(factor.T, small))
     row_corr = lax.all_gather(correction, "col", axis=0, tiled=True)
     col_corr = from_root(lax.dynamic_slice_in_dim(row_corr, offset, col_rows, 0), "row", owner)

time: 803 us -> 761 us (0.948)
  waiting for transfers between devices: 744 us -> 701 us
    psum x1 -> x2, waiting for transfers between devices: 253 us -> 210 us  [the longest x1 146 us: per_device(): small = lax.psum(one_axis, 'col')]
    unnamed x7 -> x8, waiting for transfers between devices: 216 us -> 216 us
  transfers between devices with their start and end apart: 6 -> 7, of which waited for: 6 -> 7; matrix products, arithmetic and copies ran while one was open for 2% -> 2% of each run, Pallas kernels for 0% -> 0%
where the time goes in v1:
time: 761 us; the launch traced here: 760 us
  waiting for transfers between devices  701 us (92%)
  matrix products  27.9 us (4%)
  between operations  14.2 us (2%)
  local copies, waits for them, and re-layouts  12.6 us (2%)
    unnamed x8, waiting for transfers between devices  216 us
    psum x1, waiting for transfers between devices, per_device(): small = lax.psum(one_axis, 'col')  146 us
    psum x2, waiting for transfers between devices, from_root(): return lax.psum(kept, axis)  123 us
    all_gather x1, waiting for transfers between devices, per_device(): row_panel = lax.all_gather(panel, 'col', axis=0, tiled=True)  82.3 us
    all_gather x1, waiting for transfers between devices, per_device(): row_corr = lax.all_gather(correction, 'col', axis=0, tiled=True)  70.4 us
    psum x1, waiting for transfers between devices, per_device(): one_axis = lax.psum(mult(panel.T, scaled), 'row')  64.5 us
    dot_general x7, matrix products, mult(): jnp.dot(left, right, precision=lax.Precision.HIGHEST, preferred_element_t...  27.9 us
  transfers between devices with their start and end apart: 7, of which 7 were waited for; matrix products, arithmetic and copies ran while one was open for 2% of the time, Pallas kernels for 0%

profile of v1, /device:TPU:8, one launch (start us, length us, event | category | flops | bytes accessed | tf_op | source)
XLA Modules:
  0.0 760.2 jit_solution(13323789430808149989)
XLA Ops:
  7.2 0.0 copy-start
  7.2 0.0 all-gather.3.cloned.1.call-start
  7.2 0.7 all-gather.3.cloned.1.call-update
  7.9 0.0 all-reduce.5.cloned.1.call-start
  8.0 82.3 %all-gather.3.cloned.1.call-done = f32[2048,256]{1,0:T(8,128)} async-done(((f32[64,256]{1,0:T(8,128)}), f32[2048,256]{1,0:T(8,128)}) %all-gather.3.cloned.1.call-update) | async-done | bytes 2097168 | tf_op jit(solution)/shard_map/all_gather | solution.py:24
  90.3 1.9 dynamic-slice_select_fusion.1
  92.1 0.0 all-reduce.5.cloned.1.call-update
  92.2 0.0 reduce-scatter.4.cloned.1.call-start
  92.2 65.1 %all-reduce.5.cloned.1.call-done = f32[512,256]{1,0:T(8,128)} async-done(((f32[512,256]{1,0:T(8,128)}), f32[512,256]{1,0:T(8,128)}) %all-reduce.5.cloned.1.call-update) | async-done | bytes 524304 | tf_op jit(solution)/shard_map/psum | solution.py:9
  157.3 8.7 %convolution_bitcast_fusion = f32[2048,256]{0,1:T(8,128)S(1)} fusion(f32[512,256]{1,0:T(8,128)} %all-reduce.5.cloned.1.call-done, f32[2048,512]{1,0:T(8,128)} %param.3), kind=kOutput, calls=%fused_computation.2 | convolution fusion | flops 3221225472 | bytes 6815744 | tf_op jit(solution)/shard_map/dot_general | solution.py:13
  166.0 0.0 copy-start.3
  166.0 1.8 copy.12
  167.8 0.0 reduce-scatter.4.cloned.1.call-update
  167.8 0.0 all-reduce.7.cloned.1.call-start
  167.9 214.8 %reduce-scatter.4.cloned.1.call-done = f32[64,256]{1,0:T(8,128)} async-done(((f32[2048,256]{1,0:T(8,128)}), f32[64,256]{1,0:T(8,128)}) %reduce-scatter.4.cloned.1.call-update) | async-done | bytes 65552
  382.7 0.0 copy-done
  382.7 1.1 fusion.3
  383.8 0.0 copy-done.3
  383.8 1.1 convolution_bitcast_fusion.1
  384.9 0.0 all-reduce.7.cloned.1.call-update
  384.9 0.0 all-reduce.9.cloned.1.call-start
  385.0 64.5 %all-reduce.7.cloned.1.call-done = f32[256,256]{0,1:T(8,128)} async-done(((f32[256,256]{0,1:T(8,128)}), f32[256,256]{0,1:T(8,128)}) %all-reduce.7.cloned.1.call-update) | async-done | bytes 262160 | tf_op jit(solution)/shard_map/psum | solution.py:28
  449.5 0.0 all-reduce.9.cloned.1.call-update
  449.5 0.0 all-gather.5.cloned.1.call-start
  449.6 145.9 %all-reduce.9.cloned.1.call-done = f32[256,256]{0,1:T(8,128)} async-done(((f32[256,256]{0,1:T(8,128)}), f32[256,256]{0,1:T(8,128)}) %all-reduce.9.cloned.1.call-update) | async-done | bytes 262160 | tf_op jit(solution)/shard_map/psum | solution.py:29
  595.5 1.3 fusion.4
  596.8 1.0 fusion.2
  597.8 0.0 all-gather.5.cloned.1.call-update
  597.8 0.0 copy-start.2
  597.8 0.0 all-reduce.11.cloned.1.call-start
  597.9 5.4 copy.8
  603.3 0.0 copy-start.1
  603.3 70.4 %all-gather.5.cloned.1.call-done = f32[2048,256]{1,0:T(8,128)} async-done(((f32[64,256]{1,0:T(8,128)}), f32[2048,256]{1,0:T(8,128)}) %all-gather.5.cloned.1.call-update) | async-done | bytes 2097168 | tf_op jit(solution)/shard_map/all_gather | solution.py:31
  673.7 1.9 dynamic-slice_select_fusion
  675.6 0.0 all-reduce.11.cloned.1.call-update
  675.6 0.0 copy-done.2
  675.6 6.9 fusion.5
  682.6 57.7 %all-reduce.11.cloned.1.call-done = f32[512,256]{1,0:T(8,128)} async-done(((f32[512,256]{1,0:T(8,128)}), f32[512,256]{1,0:T(8,128)}) %all-reduce.11.cloned.1.call-update) | async-done | bytes 524304 | tf_op jit(solution)/shard_map/psum | solution.py:9
  740.3 0.0 copy-done.1
  740.3 7.7 %fusion = f32[2048,512]{0,1:T(8,128)} fusion(f32[2048,512]{0,1:T(8,128)} %fusion.5, f32[2048,512]{0,1:T(8,128)} %copy.8, f32[512,256]{1,0:T(8,128)} %all-reduce.11.cloned.1.call-done, f32[2048,256]{1,0:T(8,128)S(1)} %copy-done.1), kind=kOutput, calls=%fused_computation.1 | convolution fusion | flops 3223322624 | bytes 15204352 | tf_op jit(solution)/shard_map/dot_general | solution.py:13
  748.0 5.3 copy.10
Async XLA Ops:
  7.2 375.5 %copy-start = (f32[256,256]{1,0:T(8,128)S(1)}, f32[256,256]{1,0:T(8,128)}, u32[]{:S(2)}) copy-start(f32[256,256]{1,0:T(8,128)} %param.5) | copy-start | bytes 786436
  7.2 83.1 %all-gather.3.cloned.1.call-start = ((), (), s32[]{:S(2)}) async-start(), calls=%async_computation.1 | async-start | bytes 2162688 | tf_op jit(solution)/shard_map/all_gather | solution.py:24
  7.9 149.4 %all-reduce.5.cloned.1.call-start = ((), (), s32[]{:S(2)}) async-start(), calls=%async_computation.2 | async-start | bytes 1048576 | tf_op jit(solution)/shard_map/psum | solution.py:9
  92.2 290.5 %reduce-scatter.4.cloned.1.call-start = ((), (), s32[]{:S(2)}) async-start(), calls=%async_computation.7 | async-start | bytes 2162688
  166.0 217.8 %copy-start.3 = (f32[64,256]{1,0:T(8,128)S(1)}, f32[64,256]{1,0:T(8,128)}, u32[]{:S(2)}) copy-start(f32[64,256]{1,0:T(8,128)} %param.4) | copy-start | bytes 196612
  167.8 281.7 %all-reduce.7.cloned.1.call-start = ((), (), s32[]{:S(2)}) async-start(), calls=%async_computation.3 | async-start | bytes 524288 | tf_op jit(solution)/shard_map/psum | solution.py:28
  384.9 210.5 %all-reduce.9.cloned.1.call-start = ((), (), s32[]{:S(2)}) async-start(), calls=%async_computation.4 | async-start | bytes 524288 | tf_op jit(solution)/shard_map/psum | solution.py:29
  449.5 224.2 %all-gather.5.cloned.1.call-start = ((), (), s32[]{:S(2)}) async-start(), calls=%async_computation.5 | async-start | bytes 2162688 | tf_op jit(solution)/shard_map/all_gather | solution.py:31
  597.8 77.8 %copy-start.2 = (f32[512,256]{1,0:T(8,128)S(1)}, f32[512,256]{1,0:T(8,128)}, u32[]{:S(2)}) copy-start(f32[512,256]{1,0:T(8,128)} %all-reduce.5.cloned.1.call-done) | copy-start | bytes 1572868
  597.8 142.5 %all-reduce.11.cloned.1.call-start = ((), (), s32[]{:S(2)}) async-start(), calls=%async_computation.6 | async-start | bytes 1048576 | tf_op jit(solution)/shard_map/psum | solution.py:9
  603.3 137.0 %copy-start.1 = (f32[2048,256]{1,0:T(8,128)S(1)}, f32[2048,256]{1,0:T(8,128)}, u32[]{:S(2)}) copy-start(f32[2048,256]{1,0:T(8,128)} %all-gather.3.cloned.1.call-done) | copy-start | bytes 6291460
Sparse Core Ops, SparseCore 0:
  10.6 79.6 all-gather.2
  93.2 64.0 all-reduce.4
  168.0 214.6 reduce-scatter.3
  385.4 64.0 all-reduce.6
  453.2 142.2 all-reduce.8
  598.8 74.8 all-gather.4
  676.2 64.0 all-reduce.10
